TPU v7x, 256 devices: a whole 4x4x8 slice. The times are simulated.
256 devices in a mesh: mem: 32 (over z, x), space: 8 (over y, core).
Axes of the slice: x: 4, y: 4, z: 8, core: 2. Of those that a mesh axis runs over, the one named last changes fastest.
Arguments:
- params: float32 [256, 16, 16, 384], P('mem', 'space'), may hold values from -6 to 6
- start_field: float32 [16, 16, 384], P('space'), may hold values from -6 to 6
- obs_index: int32 [8192], P('space'), may hold values from 0 to 12287
- observed: float32 [8192], P('space'), may hold values from -16 to 16
- obs_noise: float32 [256, 8192], P('mem', 'space'), may hold values from -6 to 6
Outputs:
- updated: float32 [256, 16, 16, 384], P('mem', 'space')
- predicted: float32 [256, 8192], P('mem', 'space')
Inputs may be any that keep to these rules, and one draw needn't show every extreme that they name: `obs_index`: each entry is the position, row by level by column, of a cell within the 2 rows of its own block; cells may repeat.
All inputs are finite; a program needn't handle non-finite values.
Results may differ from a plain program's by a relative error of at most 0.00025.
Values sent between devices are 32-bit elements; how exact they have to be, the bound alone decides.
A program may use at most 64 MiB of HBM per device.

v0:
```python
import jax
import jax.numpy as jnp
from jax import lax
from jax.sharding import PartitionSpec as P

obs_variance = 0.02
step_weight = 0.25


def extended(cells, sides, width):
    for axis, dim in sides:
        count = lax.axis_size(axis)
        ends = count - 1
        head = lax.slice_in_dim(cells, 0, width, axis=dim)
        tail = lax.slice_in_dim(cells, cells.shape[dim] - width, cells.shape[dim], axis=dim)
        cells = jnp.concatenate(
            [
                lax.ppermute(tail, axis, [(i, (i + 1) % count) for i in range(ends)]),
                cells,
                lax.ppermute(head, axis, [((i + 1) % count, i) for i in range(ends)]),
            ],
            axis=dim,
        )
    return cells


def advance(padded, diffusivity):
    center = padded[:, 1:-1]
    col_padded = jnp.pad(center, ((0, 0), (0, 0), (0, 0), (1, 1)))
    laplace_sum = (
        padded[:, 2:] + padded[:, :-2] + col_padded[..., 2:] + col_padded[..., :-2] - 4.0 * center
    )
    return center + step_weight * diffusivity * laplace_sum


def product(left, right):
    return jnp.dot(left, right, precision=lax.Precision.HIGHEST, preferred_element_type=jnp.float32)


def per_device(params, start_field, obs_index, observed, obs_noise):
    mem_local = params.shape[0]
    members = mem_local * lax.axis_size("mem")
    nobs_all = observed.shape[0] * lax.axis_size("space")
    diffusivity = 0.1 + 0.8 * jax.nn.sigmoid(params)
    start_pad = extended(start_field, (("space", 0),), 1)
    first_step = advance(start_pad[None], diffusivity)
    first_pad = extended(first_step, (("space", 1),), 1)
    second = advance(first_pad, diffusivity)
    predicted = second.reshape(mem_local, -1)[:, obs_index]
    misfit = observed[None, :] + obs_noise - predicted
    pred_all, misfit_all = (
        lax.all_gather(predicted, "mem", axis=0, tiled=True),
        lax.all_gather(misfit, "mem", axis=0, tiled=True),
    )
    spread_all = pred_all - jnp.mean(pred_all, axis=0)
    lead_row = lax.axis_index("mem") * mem_local
    spread_own = lax.dynamic_slice_in_dim(spread_all, lead_row, mem_local, 0)
    rows_aa, rows_ad = lax.psum(
        (product(spread_own, spread_all.T), product(spread_own, misfit_all.T)), "space"
    )
    gram_aa, gram_ad = (
        lax.all_gather(rows_aa, "mem", axis=0, tiled=True),
        lax.all_gather(rows_ad, "mem", axis=0, tiled=True),
    )
    factor = jnp.linalg.cholesky(
        gram_aa / nobs_all + obs_variance * jnp.eye(members, dtype=jnp.float32)
    )
    weights = jax.scipy.linalg.cho_solve((factor, True), gram_ad / nobs_all)
    flat_params = params.reshape(mem_local, -1)
    own_cols = lax.dynamic_slice_in_dim(weights, lead_row, mem_local, 1)
    shifted = product(own_cols.T, lax.all_gather(flat_params, "mem", axis=0, tiled=True))
    updated = params + shifted.reshape(params.shape)
    return (updated, predicted)


def solution(mesh):
    in_specs = (
        P("mem", "space", None, None),
        P("space", None, None),
        P("space"),
        P("space"),
        P("mem", "space"),
    )
    out_specs = (P("mem", "space", None, None), P("mem", "space"))
    return jax.shard_map(
        per_device, mesh=mesh, in_specs=in_specs, out_specs=out_specs, check_vma=False
    )
```

profile of v0, /device:TPU:2, one launch (start us, length us, event | category | flops | bytes accessed | tf_op | source)
XLA Modules:
  0.0 396.2 jit_solution(32803249334153336)
XLA Ops:
  7.2 0.8 fusion.36
  8.0 1.7 collective-permute-start
  9.7 1.3 collective-permute-start.1
  11.0 3.1 collective-permute-done.1
  14.2 0.8 maximum_bitcast_fusion
  15.1 1.1 multiply_add_fusion
  16.2 1.3 collective-permute-start.2
  17.5 5.1 %collective-permute-start.3 = (f32[8,1,16,384]{3,2,1,0:T(8,128)S(1)}, f32[8,1,16,384]{3,2,1,0:T(8,128)S(1)}, u32[]{:S(2)}, u32[]{:S(2)}) collective-permute-start(f32[8,1,16,384]{3,2,1,0:T(8,128)S(1)} %get-tuple-element.39), channel_id=1, source_target_pairs={{0,1},{1,2},{2,3},{3,4},{4,5},{5,6},{6,7},{8,9},{9,10},{10,11},{11... | collective-permute-start | bytes 589832 | tf_op jit(solution)/shard_map/ppermute | solution.py:18
  22.7 0.7 fusion.29
  23.4 0.3 collective-permute-done.3
  23.7 1.3 fusion.4
  25.0 4.0 %copy.33 = f32[8,2,16,384]{0,3,2,1:T(8,128)} copy(f32[8,2,16,384]{3,2,1,0:T(8,128)S(1)} %fusion.4) | data formatting | bytes 786432 | tf_op jit(solution)/shard_map/add | solution.py:33
  29.0 5.6 %gather_fusion = f32[1024,8]{1,0:T(8,128)S(1)} fusion(f32[8,12288]{0,1:T(8,128)} %bitcast.50, s32[1024]{0:T(1024)S(1)} %fusion.29), kind=kCustom, calls=%fused_computation | custom fusion | bytes 69632 | tf_op jit(solution)/shard_map/gather | solution.py:49
  34.6 0.8 copy.34
  35.5 1.4 add_subtract_fusion
  36.9 2.0 copy.46
  39.0 78.9 %all-gather.9.cloned.1.call-done = f32[256,1024]{1,0:T(8,128)} async-done(((f32[8,1024]{1,0:T(8,128)}), f32[256,1024]{1,0:T(8,128)}) %all-gather.9.cloned.1.call-update) | async-done | bytes 1048592 | tf_op jit(solution)/shard_map/all_gather | solution.py:52
  117.8 1.3 reduce_sum.9
  119.1 1.3 broadcast_subtract_fusion
  120.5 0.9 fusion.27
  121.4 72.9 %all-gather.5.cloned.1.call-done = f32[256,1024]{1,0:T(8,128)} async-done(((f32[8,1024]{1,0:T(8,128)}), f32[256,1024]{1,0:T(8,128)}) %all-gather.5.cloned.1.call-update) | async-done | bytes 1048592 | tf_op jit(solution)/shard_map/all_gather | solution.py:53
  194.3 2.1 fusion.25
  196.4 23.6 %all-reduce.3 = (f32[8,256]{1,0:T(8,128)S(1)}, f32[8,256]{1,0:T(8,128)S(1)}) all-reduce(f32[8,256]{1,0:T(8,128)S(1)} %fusion.25, f32[8,256]{1,0:T(8,128)S(1)} %fusion.27), channel_id=1, replica_groups=mesh['mem'=32,'space'=8] {'space'}, use_global_device_ids=true, to_apply=%region_6.7 | all-reduce | flops 4096 | bytes 32768 | tf_op jit(solution)/shard_map/psum | solution.py:58
  220.0 48.8 %all_gather.16 = f32[256,256]{1,0:T(8,128)S(1)} all-gather(f32[8,256]{1,0:T(8,128)S(1)} %get-tuple-element.35), channel_id=1, replica_groups=mesh['mem'=32,'space'=8] {'mem'}, dimensions={0}, use_global_device_ids=true | all-gather | bytes 270336 | tf_op jit(solution)/shard_map/all_gather | solution.py:62
  268.8 0.1 copy.35
  269.0 0.1 copy.36
  269.2 11.7 %cholesky.49 = f32[128,128]{1,0:T(8,128)S(1)} custom-call(f32[128,128]{1,0:T(8,128)S(1)} %cholesky.115), custom_call_target="Cholesky" | custom-call | tf_op jit(solution)/shard_map/jit(cholesky)/cholesky | solution.py:65
  281.0 9.8 %custom-call.18 = f32[1,128,128]{1,2,0:T(8,128)S(1)} custom-call(f32[1,128,128]{2,1,0:T(8,128)S(1)} %get-tuple-element.43), custom_call_target="InvertDiagBlocksLowerTriangular" | custom-call | tf_op jit(solution)/shard_map/jit(cholesky)/cholesky | solution.py:65
  290.9 0.2 fusion.12
  291.2 0.3 convolution_subtract_fusion.2
  291.4 11.7 %cholesky.103 = f32[128,128]{1,0:T(8,128)S(1)} custom-call(f32[128,128]{1,0:T(8,128)S(1)} %convolution_subtract_fusion.2), custom_call_target="Cholesky" | custom-call | tf_op jit(solution)/shard_map/jit(cholesky)/cholesky | solution.py:65
  303.3 0.6 compare_reduce_fusion
  305.3 4.2 %while.1 = (s32[]{:T(128)}, f32[256,256]{0,1:T(8,128)S(1)}, s32[2,2]{1,0:T(2,128)S(1)}, f32[2,128,128]{2,1,0:T(8,128)S(1)}, s32[]{:T(128)}) while((s32[]{:T(128)}, f32[256,256]{0,1:T(8,128)S(1)}, s32[2,2]{1,0:T(2,128)S(1)}, f32[2,128,128]{2,1,0:T(8,128)S(1)}, s32[]{:T(128)}) %tuple.33), condition=%wide.while_cond, body=%wide.while_body.sunk | while | flops 2 | bytes 393321 | solution.py:68
  305.5 0.6 fusion.48
  306.1 1.3 dynamic-slice.7
  307.5 0.6 fusion.48
  308.1 1.3 dynamic-slice.7
  309.5 19.7 %custom-call.19 = f32[2,128,128]{1,2,0:T(8,128)S(1)} custom-call(f32[2,128,128]{2,1,0:T(8,128)S(1)} %get-tuple-element.9), custom_call_target="InvertDiagBlocksLowerTriangular" | custom-call | tf_op jit(solution)/shard_map/jit(_cho_solve)/triangular_solve | solution.py:68
  329.2 48.6 %all_gather.18 = f32[256,256]{1,0:T(8,128)S(1)} all-gather(f32[8,256]{1,0:T(8,128)S(1)} %get-tuple-element.34), channel_id=1, replica_groups=mesh['mem'=32,'space'=8] {'mem'}, dimensions={0}, use_global_device_ids=true | all-gather | bytes 270336 | tf_op jit(solution)/shard_map/all_gather | solution.py:63
  377.8 0.1 copy.41
  377.9 0.3 fusion.10
  378.2 0.4 convolution_subtract_fusion.1
  378.6 0.3 fusion.17
  379.0 0.3 fusion.16
  379.2 0.3 convolution_subtract_fusion
  379.5 0.3 fusion.15
  379.8 9.0 %fusion.8 = f32[8,12288]{1,0:T(8,128)S(1)} fusion(f32[256,12288]{1,0:T(8,128)} %all-gather.7.cloned.1.call-done, s32[]{:T(128)S(6)} %select_n.12, f32[128,256]{1,0:T(8,128)S(1)} %fusion.15, f32[128,256]{1,0:T(8,128)S(1)} %fusion.16), kind=kOutput, calls=%fused_computation.29 | convolution fusion | flops 301991936 | bytes 13238276 | tf_op jit(solution)/shard_map/dot_general | solution.py:37
  388.8 0.8 copy_add_fusion
  (37 shorter events, 1.1 us)
Async XLA Ops:
  7.2 110.7 %all-gather.9.cloned.1.call-start = ((), (), s32[]{:S(2)}) async-start(), calls=%async_computation.2 | async-start | bytes 1081344 | tf_op jit(solution)/shard_map/all_gather | solution.py:52
  8.0 3.0 collective-permute-start
  9.7 4.5 %collective-permute-start.1 = (f32[1,16,384]{2,1,0:T(8,128)S(1)}, f32[1,16,384]{2,1,0:T(8,128)S(1)}, u32[]{:S(2)}, u32[]{:S(2)}) collective-permute-start(f32[1,16,384]{2,1,0:T(8,128)S(1)} %get-tuple-element.45), channel_id=1, source_target_pairs={{1,0},{2,1},{3,2},{4,3},{5,4},{6,5},{7,6},{9,8},{10,9},{11,10},{12... | collective-permute-start | bytes 73736 | tf_op jit(solution)/shard_map/ppermute | solution.py:20
  16.2 7.1 %collective-permute-start.2 = (f32[8,1,16,384]{3,2,1,0:T(8,128)S(1)}, f32[8,1,16,384]{3,2,1,0:T(8,128)S(1)}, u32[]{:S(2)}, u32[]{:S(2)}) collective-permute-start(f32[8,1,16,384]{3,2,1,0:T(8,128)S(1)} %get-tuple-element.38), channel_id=1, source_target_pairs={{1,0},{2,1},{3,2},{4,3},{5,4},{6,5},{7,6},{9,8},{10,9},{11,10},{12... | collective-permute-start | bytes 589832 | tf_op jit(solution)/shard_map/ppermute | solution.py:20
  17.5 6.1 %collective-permute-start.3 = (f32[8,1,16,384]{3,2,1,0:T(8,128)S(1)}, f32[8,1,16,384]{3,2,1,0:T(8,128)S(1)}, u32[]{:S(2)}, u32[]{:S(2)}) collective-permute-start(f32[8,1,16,384]{3,2,1,0:T(8,128)S(1)} %get-tuple-element.39), channel_id=1, source_target_pairs={{0,1},{1,2},{2,3},{3,4},{4,5},{5,6},{6,7},{8,9},{9,10},{10,11},{11... | collective-permute-start | bytes 589832 | tf_op jit(solution)/shard_map/ppermute | solution.py:18
  35.4 158.9 %all-gather.5.cloned.1.call-start = ((), (), s32[]{:S(2)}) async-start(), calls=%async_computation | async-start | bytes 1081344 | tf_op jit(solution)/shard_map/all_gather | solution.py:53
  36.9 342.9 %all-gather.7.cloned.1.call-start = ((), (), s32[]{:S(2)}) async-start(), calls=%async_computation.1 | async-start | bytes 12976128 | tf_op jit(solution)/shard_map/all_gather | solution.py:71
  121.4 267.4 %copy-start = (f32[8,2,16,384]{3,2,1,0:T(8,128)S(1)}, f32[8,2,16,384]{3,2,1,0:T(8,128)}, u32[]{:S(2)}) copy-start(f32[8,2,16,384]{3,2,1,0:T(8,128)} %param.5) | copy-start | bytes 1179652
Sparse Core Ops, SparseCore 0:
  35.5 82.2 all-gather.8
  120.4 73.8 all-gather.4
  197.5 116.4 all-gather.6
where the time goes:
time: 397 us; the launch traced here: 396 us
  waiting for transfers between devices  155 us (39%)
  blocking collectives  121 us (30%)
  other arithmetic  62.7 us (16%)
  local copies, waits for them, and re-layouts  17.9 us (5%)
  between operations  15.2 us (4%)
  matrix products  14.4 us (4%)
  starting transfers between devices  9.53 us (2%)
    all_gather x1, waiting for transfers between devices, per_device(): lax.all_gather(predicted, 'mem', axis=0, tiled=True)  78.9 us
    all_gather x1, waiting for transfers between devices, per_device(): lax.all_gather(misfit, 'mem', axis=0, tiled=True)  72.9 us
    all_gather x1, blocking collectives, per_device(): lax.all_gather(rows_aa, 'mem', axis=0, tiled=True)  48.8 us
    all_gather x1, blocking collectives, per_device(): lax.all_gather(rows_ad, 'mem', axis=0, tiled=True)  48.6 us
    another operation x6, other arithmetic, per_device(): jnp.linalg.cholesky(gram_aa / nobs_all + obs_variance * jnp.eye(members,...  34 us
    psum x1, blocking collectives, per_device(): lax.psum((product(spread_own, spread_all.T), product(spread_own, misfit_a...  23.6 us
    another operation x3, other arithmetic, per_device(): weights = jax.scipy.linalg.cho_solve((factor, True), gram_ad / nobs_all)  19.7 us
    dot_general x3, matrix products, product(): jnp.dot(left, right, precision=lax.Precision.HIGHEST, preferred_element_t...  12.1 us
  transfers between devices with their start and end apart: 7, of which 4 were waited for; matrix products, arithmetic and copies ran while one was open for 18% of the time, Pallas kernels for 0%

commit v1 on v0

v1 whole, which is shorter than its diff:
```python
import functools

import jax
import jax.numpy as jnp
from jax import lax
from jax.experimental import pallas as pl
from jax.experimental.pallas import tpu as pltpu
from jax.sharding import PartitionSpec as P

obs_variance = 0.02
step_weight = 0.25
x_size = 4
F32 = jnp.float32
BF16 = jnp.bfloat16


def product(left, right, dims):
    return lax.dot_general(
        left, right, (dims, ((), ())), precision=lax.Precision.HIGHEST, preferred_element_type=F32
    )


def mm(left, right):
    return product(left, right, ((1,), (0,)))


def shifted_cols(cells, amount):
    cols = cells.shape[-1]
    axis = cells.ndim - 1
    lane = lax.broadcasted_iota(jnp.int32, cells.shape, axis)
    if amount == 1:
        return jnp.where(lane == cols - 1, 0.0, pltpu.roll(cells, cols - 1, axis))
    return jnp.where(lane == 0, 0.0, pltpu.roll(cells, 1, axis))


def spd_inverse(matrix):
    n = matrix.shape[0]
    lane = lax.broadcasted_iota(jnp.int32, (1, n), 1)
    sub = lax.broadcasted_iota(jnp.int32, (n, 1), 0)

    def block(_, work):
        for t in range(8):
            row = work[t : t + 1, :]
            inv = 1.0 / row[:, t : t + 1]
            scaled = jnp.where(lane == t, inv, row * inv)
            col = work[:, t : t + 1]
            rest = jnp.where(lane == t, 0.0, work) - col * scaled
            work = jnp.where(sub == t, scaled, rest)
        work = pltpu.roll(work, n - 8, 1)
        return jnp.concatenate([work[8:], work[:8]], axis=0)

    return lax.fori_loop(0, n // 8, block, matrix)


def kernel(
    nm, ns, nobs_all,
    params_ref, start_ref, index_ref, observed_ref, noise_ref,
    updated_ref, predicted_ref,
    pt, dev, up_p, dn_p, up_s, dn_s, first_lap, second, noise_x, pred_x, pred_all,
    part, part_x, own_s, part_s, own_g, own_d, gz, gall, dz, dall, shift, back,
    send, recv,
):
    local, planes, cols = params_ref.shape
    levels = planes // 2
    members = nm * local
    nx = x_size
    nz = nm // nx
    obs = index_ref.shape[1]
    chunk = obs // nx
    cell_planes = planes // nm
    me_mem = lax.axis_index("mem")
    me_space = lax.axis_index("space")
    me_z = me_mem // nx
    me_x = me_mem % nx

    barrier = pltpu.get_barrier_semaphore()

    def hello_mem(d, c):
        pl.semaphore_signal(barrier, inc=1, device_id={"mem": (me_mem + d) % nm})
        return c

    def hello_space(d, c):
        pl.semaphore_signal(barrier, inc=1, device_id={"space": (me_space + d) % ns})
        return c

    lax.fori_loop(1, ns, hello_space, 0)
    lax.fori_loop(1, nm, hello_mem, 0)

    for b in range(planes // 8):
        block = params_ref[:, b * 8 : (b + 1) * 8, :]
        pt[b * 8 : (b + 1) * 8] = jnp.swapaxes(block, 0, 1)

    pl.semaphore_wait(barrier, (nm - 1) + (ns - 1))

    def put(src, dst, phase, device):
        pltpu.make_async_remote_copy(
            src_ref=src, dst_ref=dst, send_sem=send.at[phase], recv_sem=recv.at[phase],
            device_id=device,
        ).start()

    def arrived(ref, phase):
        pltpu.make_async_copy(ref, ref, recv.at[phase]).wait()

    def sent(ref, phase):
        pltpu.make_async_copy(ref, ref, send.at[phase]).wait()

    below = {"space": (me_space + 1) % ns}
    above = {"space": (me_space + ns - 1) % ns}
    put(start_ref, up_s, 0, below)
    put(start_ref, dn_s, 1, above)
    put(pt.at[pl.ds(levels, levels)], up_p, 2, below)
    put(pt.at[pl.ds(0, levels)], dn_p, 3, above)

    def x_peer(d):
        peer = (me_x + d) % nx
        return peer, {"mem": me_z * nx + peer}

    def z_peer(d):
        peer = (me_z + d) % nz
        return peer, {"mem": peer * nx + me_x}

    def to_chunk(ref, peer):
        return ref.at[:, pl.ds(pl.multiple_of(peer * chunk, chunk), chunk)]

    for d in range(1, nx):
        peer, device = x_peer(d)
        put(to_chunk(noise_ref, peer), noise_x.at[me_x], 4, device)
    noise_x[me_x] = noise_ref[:, pl.ds(pl.multiple_of(me_x * chunk, chunk), chunk)]

    def send_params(d, c):
        peer = (me_mem + d) % nm
        put(
            pt.at[pl.ds(peer * cell_planes, cell_planes)],
            dev.at[me_mem],
            5,
            {"mem": peer},
        )
        return c

    lax.fori_loop(1, nm, send_params, 0)
    dev[me_mem] = pt[pl.ds(me_mem * cell_planes, cell_planes)]

    def diffusivity(cells):
        return 0.1 + 0.8 / (1.0 + jnp.exp(-cells))

    arrived(up_s, 0)
    arrived(dn_s, 1)
    has_up = me_space > 0
    has_down = me_space < ns - 1
    zero = jnp.zeros((levels, cols), F32)
    state = [
        jnp.where(has_up, up_s[0], zero),
        jnp.where(has_up, up_s[1], zero),
        start_ref[0],
        start_ref[1],
        jnp.where(has_down, dn_s[0], zero),
        jnp.where(has_down, dn_s[1], zero),
    ]
    for r in range(4):
        mid = state[r + 1]
        first_lap[0, r] = mid
        first_lap[1, r] = step_weight * (
            state[r + 2] + state[r] + shifted_cols(mid, 1) + shifted_cols(mid, -1) - 4.0 * mid
        )
    arrived(up_p, 2)
    arrived(dn_p, 3)

    for level in range(levels):
        cells = [up_p[level], pt[level], pt[levels + level], dn_p[level]]
        diffs = [diffusivity(c) for c in cells]
        firsts = [
            first_lap[0, r, level : level + 1, :] + diffs[r] * first_lap[1, r, level : level + 1, :]
            for r in range(4)
        ]
        firsts[0] = jnp.where(has_up, firsts[0], 0.0)
        firsts[3] = jnp.where(has_down, firsts[3], 0.0)
        for r in range(2):
            mid = firsts[r + 1]
            lap = firsts[r + 2] + firsts[r] + shifted_cols(mid, 1) + shifted_cols(mid, -1) - 4.0 * mid
            second[r * levels + level] = mid + step_weight * diffs[r + 1] * lap

    blocks = cols // 128
    pieces = []
    for b in range(blocks):
        block = second[:, :, b * 128 : (b + 1) * 128].reshape(planes * local, 128)
        high = block.astype(BF16)
        left = block - high.astype(F32)
        mid = left.astype(BF16)
        low = (left - mid.astype(F32)).astype(BF16)
        pieces.append(jnp.concatenate([high, mid, low], axis=1))
    for c in range(nx):
        where = index_ref[:, c * chunk : (c + 1) * chunk]
        lane_of = where % 128
        block_of = where // 128
        hot = (lax.broadcasted_iota(jnp.int32, (128, chunk), 0) == lane_of).astype(F32).astype(BF16)
        hot = jnp.concatenate([hot, hot, hot], axis=0)
        total = jnp.zeros((local, chunk), F32)
        for b in range(blocks):
            picked = jnp.dot(pieces[b], hot, preferred_element_type=F32)
            for p in range(planes):
                total = total + jnp.where(
                    block_of == p * blocks + b, picked[p * local : (p + 1) * local], 0.0
                )
        predicted_ref[:, c * chunk : (c + 1) * chunk] = total

    for d in range(1, nx):
        peer, device = x_peer(d)
        put(to_chunk(predicted_ref, peer), pred_x.at[me_x], 6, device)
    pred_x[me_x] = predicted_ref[:, pl.ds(pl.multiple_of(me_x * chunk, chunk), chunk)]
    arrived(pred_x.at[pl.ds(0, nx - 1)], 6)

    for d in range(1, nz):
        peer, device = z_peer(d)
        put(pred_x, pred_all.at[me_z], 7, device)
    pred_own = pred_x[...].reshape(nx * local, chunk)
    pred_all[me_z] = pred_x[...]
    arrived(noise_x.at[pl.ds(0, nx - 1)], 4)
    seen = observed_ref[:, pl.ds(pl.multiple_of(me_x * chunk, chunk), chunk)]
    misfit = seen + noise_x[...].reshape(nx * local, chunk) - pred_own
    arrived(pred_all.at[pl.ds(0, nz - 1)], 7)

    everyone = pred_all[...].reshape(members, chunk)
    mean = jnp.sum(everyone, axis=0, keepdims=True) * (1.0 / members)
    spread = everyone - mean
    spread_own = pred_own - mean
    rows = []
    for x in range(nx):
        rows += [spread_own[x * local : (x + 1) * local], misfit[x * local : (x + 1) * local]]
    gram = product(jnp.concatenate(rows, axis=0), spread, ((1,), (1,)))
    part[...] = gram.reshape(nx, 2 * local, members)

    for d in range(1, nx):
        peer, device = x_peer(d)
        put(part.at[peer], part_x.at[me_x], 8, device)
    part_x[me_x] = part[me_x]
    arrived(part_x.at[pl.ds(0, nx - 1)], 8)
    own_s[...] = jnp.sum(part_x[...], axis=0)

    for d in range(1, ns):
        put(own_s, part_s.at[me_space], 9, {"space": (me_space + d) % ns})
    part_s[me_space] = own_s[...]
    arrived(part_s.at[pl.ds(0, ns - 1)], 9)
    total = jnp.sum(part_s[...], axis=0) * (1.0 / nobs_all)
    own_g[...] = total[:local]
    own_d[...] = total[local:]

    for d in range(1, nz):
        peer, device = z_peer(d)
        put(own_g, gz.at[me_z], 10, device)
    for d in range(1, nz):
        peer, device = z_peer(d)
        put(own_d, dz.at[me_z], 11, device)
    gz[me_z] = own_g[...]
    dz[me_z] = own_d[...]
    arrived(gz.at[pl.ds(0, nz - 1)], 10)
    for d in range(1, nx):
        peer, device = x_peer(d)
        put(gz, gall.at[:, me_x], 12, device)
    gall[:, me_x] = gz[...]
    arrived(dz.at[pl.ds(0, nz - 1)], 11)
    for d in range(1, nx):
        peer, device = x_peer(d)
        put(dz, dall.at[:, me_x], 13, device)
    dall[:, me_x] = dz[...]

    arrived(dev.at[pl.ds(0, nm - 1)], 5)
    width = cell_planes * cols
    deviation = jnp.concatenate(
        [dev[:, p].reshape(members, cols) for p in range(cell_planes)], axis=1
    )
    deviation = deviation - jnp.sum(deviation, axis=0, keepdims=True) * (1.0 / members)

    arrived(gall.at[:, pl.ds(0, nx - 1)], 12)
    half = members // 2
    system = gall[...].reshape(members, members)
    eye = lax.broadcasted_iota(jnp.int32, (members, members), 0) == lax.broadcasted_iota(
        jnp.int32, (members, members), 1
    )
    system = system + jnp.where(eye, obs_variance, 0.0)
    upper = system[:half, half:]
    inv_a = spd_inverse(system[:half, :half])
    lower = mm(system[half:, :half], inv_a)
    inv_b = spd_inverse(system[half:, half:] - mm(lower, upper))
    dev_a, dev_b = deviation[:half], deviation[half:]
    sol_b = mm(inv_b, dev_b - mm(lower, dev_a))
    sol_a = mm(inv_a, dev_a) - product(lower, sol_b, ((0,), (0,)))
    arrived(dall.at[:, pl.ds(0, nx - 1)], 13)
    gains = dall[...].reshape(members, members)
    moved = mm(gains[:, :half], sol_a) + mm(gains[:, half:], sol_b)
    for p in range(cell_planes):
        shift[:, p] = moved[:, p * cols : (p + 1) * cols].reshape(nm, local, cols)

    def send_back(d, c):
        peer = (me_mem + d) % nm
        put(
            shift.at[peer],
            back.at[pl.ds(me_mem * cell_planes, cell_planes)],
            14,
            {"mem": peer},
        )
        return c

    lax.fori_loop(1, nm, send_back, 0)
    back[pl.ds(me_mem * cell_planes, cell_planes)] = shift[me_mem]

    sent(start_ref, 0)
    sent(start_ref, 1)
    sent(up_p, 2)
    sent(dn_p, 3)
    sent(noise_x.at[pl.ds(0, nx - 1)], 4)
    sent(dev.at[pl.ds(0, nm - 1)], 5)
    sent(pred_x.at[pl.ds(0, nx - 1)], 6)
    sent(pred_all.at[pl.ds(0, nz - 1)], 7)
    sent(part_x.at[pl.ds(0, nx - 1)], 8)
    sent(part_s.at[pl.ds(0, ns - 1)], 9)
    sent(gz.at[pl.ds(0, nz - 1)], 10)
    sent(dz.at[pl.ds(0, nz - 1)], 11)
    sent(gall.at[:, pl.ds(0, nx - 1)], 12)
    sent(dall.at[:, pl.ds(0, nx - 1)], 13)
    sent(back.at[pl.ds(0, (nm - 1) * cell_planes)], 14)

    arrived(back.at[pl.ds(0, (nm - 1) * cell_planes)], 14)
    for b in range(planes // 8):
        block = jnp.swapaxes(back[b * 8 : (b + 1) * 8], 0, 1)
        updated_ref[:, b * 8 : (b + 1) * 8, :] = params_ref[:, b * 8 : (b + 1) * 8, :] + block


def per_device(params, start_field, obs_index, observed, obs_noise):
    local, rows, levels, cols = params.shape
    nm, ns = lax.axis_size("mem"), lax.axis_size("space")
    obs = obs_index.shape[0]
    members = nm * local
    nx = x_size
    nz = nm // nx
    chunk = obs // nx
    planes = rows * levels
    cell_planes = planes // nm
    vmem = pl.BlockSpec(memory_space=pltpu.VMEM)
    shapes = [
        (planes, local, cols),
        (nm, cell_planes, local, cols),
        (levels, local, cols),
        (levels, local, cols),
        (rows, levels, cols),
        (rows, levels, cols),
        (2, 4, levels, cols),
        (planes, local, cols),
        (nx, local, chunk),
        (nx, local, chunk),
        (nz, nx, local, chunk),
        (nx, 2 * local, members),
        (nx, 2 * local, members),
        (2 * local, members),
        (ns, 2 * local, members),
        (local, members),
        (local, members),
        (nz, local, members),
        (nz, nx, local, members),
        (nz, local, members),
        (nz, nx, local, members),
        (nm, cell_planes, local, cols),
        (planes, local, cols),
    ]
    updated, predicted = pl.pallas_call(
        functools.partial(kernel, nm, ns, obs * ns),
        out_shape=(
            jax.ShapeDtypeStruct((local, planes, cols), F32),
            jax.ShapeDtypeStruct((local, obs), F32),
        ),
        in_specs=[vmem] * 5,
        out_specs=(vmem, vmem),
        scratch_shapes=[pltpu.VMEM(s, F32) for s in shapes]
        + [pltpu.SemaphoreType.DMA((15,)), pltpu.SemaphoreType.DMA((15,))],
        compiler_params=pltpu.CompilerParams(collective_id=0, has_side_effects=True),
    )(
        params.reshape(local, planes, cols),
        start_field,
        obs_index.reshape(1, obs),
        observed.reshape(1, obs),
        obs_noise,
    )
    return updated.reshape(params.shape), predicted


def solution(mesh):
    in_specs = (
        P("mem", "space", None, None),
        P("space", None, None),
        P("space"),
        P("space"),
        P("mem", "space"),
    )
    out_specs = (P("mem", "space", None, None), P("mem", "space"))
    return jax.shard_map(
        per_device, mesh=mesh, in_specs=in_specs, out_specs=out_specs, check_vma=False
    )
```

time: 397 us -> 90.1 us (0.23)
  waiting for transfers between devices: 155 us -> 0 us
  blocking collectives: 121 us -> 0 us
  Pallas kernels: 0 us -> 86.4 us
  other arithmetic: 62.7 us -> 0 us
  local copies, waits for them, and re-layouts: 17.9 us -> 2.39 us
  between operations: 15.2 us -> 0.65 us
  matrix products: 14.4 us -> 0 us
  starting transfers between devices: 9.53 us -> 0 us
    all_gather x3 -> x0, waiting for transfers between devices: 152 us -> none  [the longest x1 78.9 us: per_device(): lax.all_gather(predicted, 'mem', axis=0, tiled=True)]
    all_gather x2 -> x0, blocking collectives: 97.4 us -> none  [the longest x1 48.8 us: per_device(): lax.all_gather(rows_aa, 'mem', axis=0, tiled=True)]
    pallas_call x0 -> x1, Pallas kernels: none -> 86.4 us  [per_device(): pl.pallas_call(functools.partial(kernel, nm, ns, obs * ns), out_shape=(ja...]
    another operation x9 -> x0, other arithmetic: 53.7 us -> none  [the longest x6 34 us: per_device(): jnp.linalg.cholesky(gram_aa / nobs_all + obs_variance * jnp.eye(members,...]
    psum x1 -> x0, blocking collectives: 23.6 us -> none  [per_device(): lax.psum((product(spread_own, spread_all.T), product(spread_own, misfit_a...]
    dot_general x3 -> x0, matrix products: 12.1 us -> none  [product(): jnp.dot(left, right, precision=lax.Precision.HIGHEST, preferred_element_t...]
    ppermute x4 -> x0, starting transfers between devices: 9.41 us -> none  [the longest x2 6.83 us: extended(): lax.ppermute(tail, axis, [(i, (i + 1) % count) for i in range(ends)])]
    gather x2 -> x0, local copies, waits for them, and re-layouts: 6.37 us -> none  [per_device(): predicted = second.reshape(mem_local, -1)[:, obs_index]]
  transfers between devices with their start and end apart: 7 -> 0, of which waited for: 4 -> 0; matrix products, arithmetic and copies ran while one was open for 18% -> 0% of each run, Pallas kernels for 0% -> 0%
where the time goes in v1:
time: 90.1 us; the launch traced here: 89.5 us
  Pallas kernels  86.4 us (96%)
  local copies, waits for them, and re-layouts  2.39 us (3%)
    pallas_call x1, Pallas kernels, per_device(): pl.pallas_call(functools.partial(kernel, nm, ns, obs * ns), out_shape=(ja...  86.4 us
    unnamed x4, local copies, waits for them, and re-layouts  2.39 us

profile of v1, /device:TPU:2, one launch (start us, length us, event | category | flops | bytes accessed | tf_op | source)
XLA Modules:
  0.0 89.5 jit_solution(6489568878902229894)
XLA Ops:
  0.6 86.4 %shard_map.68 = (f32[8,32,384]{2,1,0:T(8,128)}, f32[8,1024]{1,0:T(8,128)}) custom-call(f32[8,32,384]{2,1,0:T(8,128)} %bitcast.5, f32[2,16,384]{2,1,0:T(8,128)} %start_ref.1, s32[1,1024]{1,0:T(1,128)} %bitcast.6, f32[1,1024]{1,0:T(1,128)} %bitcast.7, f32[8,1024]{1,0:T(8,128)} %noise_ref.1), custom_call_target="tpu_custom_call" | custom-call | tf_op jit(solution)/shard_map/pallas_call | solution.py:364
  87.0 0.0 copy-start
  87.1 1.8 %copy.9 = f32[8,2,16,384]{3,2,1,0:T(8,128)} copy(f32[8,2,16,384]{3,2,1,0:T(8,128)} %bitcast.4) | data formatting | bytes 786432
  88.8 0.0 copy-done
  88.8 0.6 copy.10
Async XLA Ops:
  87.0 1.8 %copy-start = (f32[8,1024]{1,0:T(8,128)S(1)}, f32[8,1024]{1,0:T(8,128)}, u32[]{:S(2)}) copy-start(f32[8,1024]{1,0:T(8,128)} %get-tuple-element.9) | copy-start | bytes 98308

commit v2 on v1

v2 whole, which is shorter than its diff:
```python
import functools

import jax
import jax.numpy as jnp
from jax import lax
from jax.experimental import pallas as pl
from jax.experimental.pallas import tpu as pltpu
from jax.sharding import PartitionSpec as P

obs_variance = 0.02
step_weight = 0.25
x_size = 4
F32 = jnp.float32
BF16 = jnp.bfloat16


def product(left, right, dims):
    return lax.dot_general(
        left, right, (dims, ((), ())), precision=lax.Precision.HIGHEST, preferred_element_type=F32
    )


def mm(left, right):
    return product(left, right, ((1,), (0,)))


def shifted_cols(cells, amount):
    cols = cells.shape[-1]
    axis = cells.ndim - 1
    lane = lax.broadcasted_iota(jnp.int32, cells.shape, axis)
    if amount == 1:
        return jnp.where(lane == cols - 1, 0.0, pltpu.roll(cells, cols - 1, axis))
    return jnp.where(lane == 0, 0.0, pltpu.roll(cells, 1, axis))


def swept_rows(rows):
    count, n = rows.shape
    sub = lax.broadcasted_iota(jnp.int32, rows.shape, 0)
    lane = lax.broadcasted_iota(jnp.int32, rows.shape, 1)
    entry = {}
    for j in range(count):
        col = jnp.broadcast_to(rows[:, j : j + 1], rows.shape)
        for i in range(j, count):
            entry[i, j] = jnp.broadcast_to(col[i : i + 1], rows.shape)

    def at(i, j):
        return entry[max(i, j), min(i, j)]

    for k in range(count):
        inv = 1.0 / entry[k, k]
        others = [i for i in range(count) if i != k]
        old = {i: at(i, k) for i in others}
        new = {i: old[i] * inv for i in others}
        for j in others:
            for i in others:
                if i >= j:
                    entry[i, j] = entry[i, j] - new[i] * old[j]
        for i in others:
            entry[max(i, k), min(i, k)] = new[i]
        entry[k, k] = -inv

    total = jnp.zeros(rows.shape, F32)
    corner = total
    for j in range(count):
        col = at(0, j)
        for i in range(1, count):
            col = jnp.where(sub == i, at(i, j), col)
        total = total - col * rows[j : j + 1]
        corner = jnp.where(lane == j, col, corner)
    return jnp.where(lane < count, corner, total)


def spd_inverse(matrix):
    n = matrix.shape[0]
    lane = lax.broadcasted_iota(jnp.int32, (1, n), 1)

    def block(_, work):
        head = swept_rows(work[:8])
        rest = work[8:]
        tail = jnp.where(lane < 8, 0.0, rest)
        for t in range(8):
            tail = tail - rest[:, t : t + 1] * head[t : t + 1]
        return jnp.concatenate([pltpu.roll(tail, n - 8, 1), pltpu.roll(head, n - 8, 1)], axis=0)

    return -lax.fori_loop(0, n // 8, block, matrix)


def kernel(
    nm, ns, nobs_all,
    params_ref, start_ref, index_ref, observed_ref, noise_ref,
    shift_ref, predicted_ref,
    pt, dev, up_p, dn_p, up_s, dn_s, first_lap, second, noise_x, pred_all,
    part_g, part_m, part_gx, part_mx, own_g, own_m, part_gs, part_ms, rows_a, rows_b, rows_m,
    gram_a, gram_b, gains_all, shift, back,
    send, recv, rounds,
):
    local, planes, cols = params_ref.shape
    levels = planes // 2
    members = nm * local
    half = members // 2
    nx = x_size
    nz = nm // nx
    obs = index_ref.shape[1]
    chunk = obs // nx
    cell_planes = planes // nm
    me_mem = lax.axis_index("mem")
    me_space = lax.axis_index("space")
    me_z = me_mem // nx
    me_x = me_mem % nx

    def space_peer(d):
        return {"space": (me_space + d) % ns}

    def x_peer(d):
        peer = (me_x + d) % nx
        return peer, {"mem": me_z * nx + peer}

    def z_peer(d):
        return {"mem": (me_z + d) % nz * nx + me_x}

    barrier = pltpu.get_barrier_semaphore()
    nearby = [space_peer(1), space_peer(ns - 1), z_peer(1), z_peer(nz - 1)]
    greeted = nearby + [x_peer(d)[1] for d in range(1, nx)]
    for device in greeted:
        pl.semaphore_signal(barrier, inc=1, device_id=device)

    for b in range(planes // 8):
        pt[b * 8 : (b + 1) * 8] = jnp.swapaxes(params_ref[:, b * 8 : (b + 1) * 8, :], 0, 1)

    pl.semaphore_wait(barrier, len(greeted))

    def put(src, dst, phase, device):
        pltpu.make_async_remote_copy(
            src_ref=src, dst_ref=dst, send_sem=send.at[phase], recv_sem=recv.at[phase],
            device_id=device,
        ).start()

    def arrived(ref, phase):
        pltpu.make_async_copy(ref, ref, recv.at[phase]).wait()

    def sent(ref, phase):
        pltpu.make_async_copy(ref, ref, send.at[phase]).wait()

    def put_all(pick, dst, phase):
        def body(t, c):
            q = t // nx
            dz = nz // 2 + (1 - 2 * (q % 2)) * ((q + 1) // 2)
            peer = (me_z + dz) % nz * nx + (me_x + t + 1) % nx
            put(pick(peer), dst, phase, {"mem": peer})
            return c

        lax.fori_loop(0, nm - 1, body, 0)

    def greet(devices, step):
        for device in devices:
            pl.semaphore_signal(rounds.at[step], inc=1, device_id=device)

    put(start_ref, up_s, 0, space_peer(1))
    put(start_ref, dn_s, 1, space_peer(ns - 1))
    put(pt.at[pl.ds(levels, levels)], up_p, 2, space_peer(1))
    put(pt.at[pl.ds(0, levels)], dn_p, 3, space_peer(ns - 1))
    greet(nearby, 0)

    def to_chunk(ref, peer):
        return ref.at[:, pl.ds(pl.multiple_of(peer * chunk, chunk), chunk)]

    for d in range(1, nx):
        peer, device = x_peer(d)
        put(to_chunk(noise_ref, peer), noise_x.at[me_x], 4, device)
    noise_x[me_x] = noise_ref[:, pl.ds(pl.multiple_of(me_x * chunk, chunk), chunk)]
    dev[me_mem] = pt[pl.ds(me_mem * cell_planes, cell_planes)]

    pl.semaphore_wait(rounds.at[0], 4)
    greet([space_peer(2), space_peer(ns - 2), z_peer(2), z_peer(nz - 2)], 1)

    def diffusivity(cells):
        return 0.1 + 0.8 / (1.0 + jnp.exp(-cells))

    arrived(up_s, 0)
    arrived(dn_s, 1)
    has_up = me_space > 0
    has_down = me_space < ns - 1
    zero = jnp.zeros((levels, cols), F32)
    state = [
        jnp.where(has_up, up_s[0], zero),
        jnp.where(has_up, up_s[1], zero),
        start_ref[0],
        start_ref[1],
        jnp.where(has_down, dn_s[0], zero),
        jnp.where(has_down, dn_s[1], zero),
    ]
    for r in range(4):
        mid = state[r + 1]
        first_lap[0, r] = mid
        first_lap[1, r] = step_weight * (
            state[r + 2] + state[r] + shifted_cols(mid, 1) + shifted_cols(mid, -1) - 4.0 * mid
        )
    pl.semaphore_wait(rounds.at[1], 4)
    greet([z_peer(nz // 2)], 2)
    arrived(up_p, 2)
    arrived(dn_p, 3)

    for level in range(levels):
        cells = [up_p[level], pt[level], pt[levels + level], dn_p[level]]
        diffs = [diffusivity(c) for c in cells]
        firsts = [
            first_lap[0, r, level : level + 1, :] + diffs[r] * first_lap[1, r, level : level + 1, :]
            for r in range(4)
        ]
        firsts[0] = jnp.where(has_up, firsts[0], 0.0)
        firsts[3] = jnp.where(has_down, firsts[3], 0.0)
        for r in range(2):
            mid = firsts[r + 1]
            lap = firsts[r + 2] + firsts[r] + shifted_cols(mid, 1) + shifted_cols(mid, -1) - 4.0 * mid
            second[r * levels + level] = mid + step_weight * diffs[r + 1] * lap

    blocks = cols // 128
    pieces = []
    for b in range(blocks):
        block = second[:, :, b * 128 : (b + 1) * 128].reshape(planes * local, 128)
        high = block.astype(BF16)
        left = block - high.astype(F32)
        mid = left.astype(BF16)
        low = (left - mid.astype(F32)).astype(BF16)
        pieces.append(jnp.concatenate([high, mid, low], axis=1))
    for c in range(nx):
        where = index_ref[:, c * chunk : (c + 1) * chunk]
        lane_of = where % 128
        block_of = where // 128
        hot = (lax.broadcasted_iota(jnp.int32, (128, chunk), 0) == lane_of).astype(F32).astype(BF16)
        hot = jnp.concatenate([hot, hot, hot], axis=0)
        total = jnp.zeros((local, chunk), F32)
        for b in range(blocks):
            picked = jnp.dot(pieces[b], hot, preferred_element_type=F32)
            for p in range(planes):
                total = total + jnp.where(
                    block_of == p * blocks + b, picked[p * local : (p + 1) * local], 0.0
                )
        predicted_ref[:, c * chunk : (c + 1) * chunk] = total

    pl.semaphore_wait(rounds.at[2], 1)
    put_all(lambda peer: to_chunk(predicted_ref, peer % nx), pred_all.at[me_mem], 5)
    pred_all[me_mem] = predicted_ref[:, pl.ds(pl.multiple_of(me_x * chunk, chunk), chunk)]
    arrived(noise_x.at[pl.ds(0, nx - 1)], 4)
    seen = observed_ref[:, pl.ds(pl.multiple_of(me_x * chunk, chunk), chunk)]
    target = seen + noise_x[...].reshape(nx * local, chunk)
    arrived(pred_all.at[pl.ds(0, nm - 1)], 5)

    everyone = pred_all[...].reshape(members, chunk)
    pred_own = pred_all[pl.ds(me_z * nx, nx)].reshape(nx * local, chunk)
    mean = jnp.sum(everyone, axis=0, keepdims=True) * (1.0 / members)
    spread = everyone - mean
    part_g[...] = product(pred_own - mean, spread, ((1,), (1,))).reshape(nx, local, members)
    for d in range(1, nx):
        peer, device = x_peer(d)
        put(part_g.at[peer], part_gx.at[me_x], 6, device)
    part_m[...] = product(target - pred_own, spread, ((1,), (1,))).reshape(nx, local, members)
    for d in range(1, nx):
        peer, device = x_peer(d)
        put(part_m.at[peer], part_mx.at[me_x], 7, device)
    part_gx[me_x] = part_g[me_x]
    part_mx[me_x] = part_m[me_x]

    arrived(part_gx.at[pl.ds(0, nx - 1)], 6)
    own_g[...] = jnp.sum(part_gx[...], axis=0)
    for d in range(1, ns):
        put(own_g, part_gs.at[me_space], 8, space_peer(d))
    part_gs[me_space] = own_g[...]
    arrived(part_mx.at[pl.ds(0, nx - 1)], 7)
    own_m[...] = jnp.sum(part_mx[...], axis=0)
    for d in range(1, ns):
        put(own_m, part_ms.at[me_space], 9, space_peer(d))
    part_ms[me_space] = own_m[...]

    arrived(part_gs.at[pl.ds(0, ns - 1)], 8)
    total = jnp.sum(part_gs[...], axis=0) * (1.0 / nobs_all)
    rows_a[...] = total[:, :half]
    rows_b[...] = total[:, half:]
    leading = me_z < nz // 2

    @pl.when(leading)
    def _():
        put_all(lambda peer: rows_a, gram_a.at[me_mem], 10)
        gram_a[me_mem] = rows_a[...]

    put_all(lambda peer: rows_b, gram_b.at[me_mem], 11)
    gram_b[me_mem] = rows_b[...]

    arrived(part_ms.at[pl.ds(0, ns - 1)], 9)
    rows_m[...] = jnp.sum(part_ms[...], axis=0) * (1.0 / nobs_all)
    put_all(lambda peer: rows_m, gains_all.at[me_mem], 12)
    gains_all[me_mem] = rows_m[...]
    put_all(lambda peer: pt.at[pl.ds(peer * cell_planes, cell_planes)], dev.at[me_mem], 13)

    @pl.when(leading)
    def _():
        arrived(gram_a.at[pl.ds(0, nm // 2 - 1)], 10)

    @pl.when(jnp.logical_not(leading))
    def _():
        arrived(gram_a, 10)

    eye = lax.broadcasted_iota(jnp.int32, (half, half), 0) == lax.broadcasted_iota(
        jnp.int32, (half, half), 1
    )
    ridge = jnp.where(eye, obs_variance, 0.0)
    inv_a = spd_inverse(gram_a[...].reshape(half, half) + ridge)
    arrived(gram_b.at[pl.ds(0, nm - 1)], 11)
    right = gram_b[...].reshape(members, half)
    upper = right[:half]
    lower = product(upper, inv_a, ((0,), (0,)))
    inv_b = spd_inverse(right[half:] + ridge - mm(lower, upper))

    arrived(dev.at[pl.ds(0, nm - 1)], 13)
    deviation = jnp.concatenate(
        [dev[:, p].reshape(members, cols) for p in range(cell_planes)], axis=1
    )
    deviation = deviation - jnp.sum(deviation, axis=0, keepdims=True) * (1.0 / members)
    dev_a, dev_b = deviation[:half], deviation[half:]
    sol_b = mm(inv_b, dev_b - mm(lower, dev_a))
    sol_a = mm(inv_a, dev_a) - product(lower, sol_b, ((0,), (0,)))
    arrived(gains_all.at[pl.ds(0, nm - 1)], 12)
    gains = gains_all[...].reshape(members, members)
    moved = mm(gains[:, :half], sol_a) + mm(gains[:, half:], sol_b)
    for p in range(cell_planes):
        shift[:, p] = moved[:, p * cols : (p + 1) * cols].reshape(nm, local, cols)

    put_all(lambda peer: shift.at[peer], back.at[pl.ds(me_mem * cell_planes, cell_planes)], 14)
    back[pl.ds(me_mem * cell_planes, cell_planes)] = shift[me_mem]

    sent(start_ref, 0)
    sent(start_ref, 1)
    sent(up_p, 2)
    sent(dn_p, 3)
    sent(noise_x.at[pl.ds(0, nx - 1)], 4)
    sent(pred_all.at[pl.ds(0, nm - 1)], 5)
    sent(part_gx.at[pl.ds(0, nx - 1)], 6)
    sent(part_mx.at[pl.ds(0, nx - 1)], 7)
    sent(part_gs.at[pl.ds(0, ns - 1)], 8)
    sent(part_ms.at[pl.ds(0, ns - 1)], 9)

    @pl.when(leading)
    def _():
        sent(gram_b.at[pl.ds(0, nm - 1)], 10)

    sent(gram_b.at[pl.ds(0, nm - 1)], 11)
    sent(gains_all.at[pl.ds(0, nm - 1)], 12)
    sent(dev.at[pl.ds(0, nm - 1)], 13)
    sent(back.at[pl.ds(0, (nm - 1) * cell_planes)], 14)

    arrived(back.at[pl.ds(0, (nm - 1) * cell_planes)], 14)
    for b in range(planes // 8):
        shift_ref[:, b * 8 : (b + 1) * 8, :] = jnp.swapaxes(back[b * 8 : (b + 1) * 8], 0, 1)


def per_device(params, start_field, obs_index, observed, obs_noise):
    local, rows, levels, cols = params.shape
    nm, ns = lax.axis_size("mem"), lax.axis_size("space")
    obs = obs_index.shape[0]
    members = nm * local
    nx = x_size
    chunk = obs // nx
    planes = rows * levels
    cell_planes = planes // nm
    vmem = pl.BlockSpec(memory_space=pltpu.VMEM)
    half = members // 2
    shapes = [
        (planes, local, cols),
        (nm, cell_planes, local, cols),
        (levels, local, cols),
        (levels, local, cols),
        (rows, levels, cols),
        (rows, levels, cols),
        (2, 4, levels, cols),
        (planes, local, cols),
        (nx, local, chunk),
        (nm, local, chunk),
        (nx, local, members),
        (nx, local, members),
        (nx, local, members),
        (nx, local, members),
        (local, members),
        (local, members),
        (ns, local, members),
        (ns, local, members),
        (local, half),
        (local, half),
        (local, members),
        (nm // 2, local, half),
        (nm, local, half),
        (nm, local, members),
        (nm, cell_planes, local, cols),
        (planes, local, cols),
    ]
    shift, predicted = pl.pallas_call(
        functools.partial(kernel, nm, ns, obs * ns),
        out_shape=(
            jax.ShapeDtypeStruct((local, planes, cols), F32),
            jax.ShapeDtypeStruct((local, obs), F32),
        ),
        in_specs=[vmem] * 5,
        out_specs=(vmem, vmem),
        scratch_shapes=[pltpu.VMEM(s, F32) for s in shapes]
        + [pltpu.SemaphoreType.DMA((15,)), pltpu.SemaphoreType.DMA((15,)), pltpu.SemaphoreType.REGULAR((3,))],
        compiler_params=pltpu.CompilerParams(collective_id=0, has_side_effects=True),
    )(
        params.reshape(local, planes, cols),
        start_field,
        obs_index.reshape(1, obs),
        observed.reshape(1, obs),
        obs_noise,
    )
    return params + shift.reshape(params.shape), predicted


def solution(mesh):
    in_specs = (
        P("mem", "space", None, None),
        P("space", None, None),
        P("space"),
        P("space"),
        P("mem", "space"),
    )
    out_specs = (P("mem", "space", None, None), P("mem", "space"))
    return jax.shard_map(
        per_device, mesh=mesh, in_specs=in_specs, out_specs=out_specs, check_vma=False
    )
```

time: 90.1 us -> 72.4 us (0.80)
  Pallas kernels: 86.4 us -> 69 us
  other arithmetic: 0 us -> 1.79 us
  local copies, waits for them, and re-layouts: 2.39 us -> 0.62 us
    pallas_call x1, Pallas kernels: 86.4 us -> 69 us  [per_device(): pl.pallas_call(functools.partial(kernel, nm, ns, obs * ns), out_shape=(ja...]
    add x0 -> x1, other arithmetic: none -> 1.79 us  [per_device(): return (params + shift.reshape(params.shape), predicted)]
    unnamed x4 -> x5, local copies, waits for them, and re-layouts: 2.39 us -> 0.62 us
where the time goes in v2:
time: 72.4 us; the launch traced here: 72.1 us
  Pallas kernels  69 us (95%)
  other arithmetic  1.79 us (2%)
    pallas_call x1, Pallas kernels, per_device(): pl.pallas_call(functools.partial(kernel, nm, ns, obs * ns), out_shape=(ja...  69 us
    add x1, other arithmetic, per_device(): return (params + shift.reshape(params.shape), predicted)  1.79 us

profile of v2, /device:TPU:2, one launch (start us, length us, event | category | flops | bytes accessed | tf_op | source)
XLA Modules:
  0.0 72.1 jit_solution(197840875588241681)
XLA Ops:
  0.6 0.0 copy-start
  0.6 69.0 %shard_map.68 = (f32[8,32,384]{2,1,0:T(8,128)}, f32[8,1024]{1,0:T(8,128)}) custom-call(f32[8,32,384]{2,1,0:T(8,128)} %bitcast.4, f32[2,16,384]{2,1,0:T(8,128)} %start_ref.1, s32[1,1024]{1,0:T(1,128)} %bitcast.6, f32[1,1024]{1,0:T(1,128)} %bitcast.7, f32[8,1024]{1,0:T(8,128)} %noise_ref.1), custom_call_target="tpu_custom_call" | custom-call | tf_op jit(solution)/shard_map/pallas_call | solution.py:395
  69.7 0.0 copy-done
  69.7 0.0 copy-start.1
  69.7 1.8 %add.3 = f32[8,2,16,384]{3,2,1,0:T(8,128)} add(f32[8,2,16,384]{3,2,1,0:T(8,128)S(1)} %copy-done, f32[8,2,16,384]{3,2,1,0:T(8,128)} %bitcast.5) | non-fusion elementwise | flops 98304 | bytes 1179648 | tf_op jit(solution)/shard_map/add | solution.py:413
  71.5 0.0 copy-done.1
  71.5 0.6 copy.8
Async XLA Ops:
  0.6 69.1 %copy-start = (f32[8,2,16,384]{3,2,1,0:T(8,128)S(1)}, f32[8,2,16,384]{3,2,1,0:T(8,128)}, u32[]{:S(2)}) copy-start(f32[8,2,16,384]{3,2,1,0:T(8,128)} %param.5) | copy-start | bytes 1179652
  69.7 1.8 %copy-start.1 = (f32[8,1024]{1,0:T(8,128)S(1)}, f32[8,1024]{1,0:T(8,128)}, u32[]{:S(2)}) copy-start(f32[8,1024]{1,0:T(8,128)} %get-tuple-element.9) | copy-start | bytes 98308

commit v3 on v2

--- a/solution.py
+++ b/solution.py
@@ -149,7 +149,7 @@
             put(pick(peer), dst, phase, {"mem": peer})
             return c
 
-        lax.fori_loop(0, nm - 1, body, 0)
+        lax.fori_loop(0, nm - 1, body, 0, unroll=True)
 
     def greet(devices, step):
         for device in devices:
@@ -196,7 +196,7 @@
             state[r + 2] + state[r] + shifted_cols(mid, 1) + shifted_cols(mid, -1) - 4.0 * mid
         )
     pl.semaphore_wait(rounds.at[1], 4)
-    greet([z_peer(nz // 2)], 2)
+    greet([x_peer(d)[1] for d in range(1, nx)], 2)
     arrived(up_p, 2)
     arrived(dn_p, 3)
 
@@ -238,7 +238,7 @@
                 )
         predicted_ref[:, c * chunk : (c + 1) * chunk] = total
 
-    pl.semaphore_wait(rounds.at[2], 1)
+    pl.semaphore_wait(rounds.at[2], nx - 1)
     put_all(lambda peer: to_chunk(predicted_ref, peer % nx), pred_all.at[me_mem], 5)
     pred_all[me_mem] = predicted_ref[:, pl.ds(pl.multiple_of(me_x * chunk, chunk), chunk)]
     arrived(noise_x.at[pl.ds(0, nx - 1)], 4)
@@ -258,6 +258,7 @@
     for d in range(1, nx):
         peer, device = x_peer(d)
         put(part_m.at[peer], part_mx.at[me_x], 7, device)
+    put_all(lambda peer: pt.at[pl.ds(peer * cell_planes, cell_planes)], dev.at[me_mem], 13)
     part_gx[me_x] = part_g[me_x]
     part_mx[me_x] = part_m[me_x]
 
@@ -290,7 +291,6 @@
     rows_m[...] = jnp.sum(part_ms[...], axis=0) * (1.0 / nobs_all)
     put_all(lambda peer: rows_m, gains_all.at[me_mem], 12)
     gains_all[me_mem] = rows_m[...]
-    put_all(lambda peer: pt.at[pl.ds(peer * cell_planes, cell_planes)], dev.at[me_mem], 13)
 
     @pl.when(leading)
     def _():

time: 72.4 us -> 68.3 us (0.943); the launches traced: 72.1 us -> 67.1 us
  Pallas kernels: 69 us -> 64 us
    pallas_call x1, Pallas kernels: 69 us -> 64 us  [per_device(): pl.pallas_call(functools.partial(kernel, nm, ns, obs * ns), out_shape=(ja...]
where the time goes in v3:
time: 68.3 us; the launch traced here: 67.1 us
  Pallas kernels  64 us (94%)
  other arithmetic  1.79 us (3%)
    pallas_call x1, Pallas kernels, per_device(): pl.pallas_call(functools.partial(kernel, nm, ns, obs * ns), out_shape=(ja...  64 us
    add x1, other arithmetic, per_device(): return (params + shift.reshape(params.shape), predicted)  1.79 us

profile of v3, /device:TPU:2, one launch (start us, length us, event | category | flops | bytes accessed | tf_op | source)
XLA Modules:
  0.0 67.1 jit_solution(14865899757178789833)
XLA Ops:
  0.6 0.0 copy-start
  0.6 64.0 %shard_map.68 = (f32[8,32,384]{2,1,0:T(8,128)}, f32[8,1024]{1,0:T(8,128)}) custom-call(f32[8,32,384]{2,1,0:T(8,128)} %bitcast.4, f32[2,16,384]{2,1,0:T(8,128)} %start_ref.1, s32[1,1024]{1,0:T(1,128)} %bitcast.6, f32[1,1024]{1,0:T(1,128)} %bitcast.7, f32[8,1024]{1,0:T(8,128)} %noise_ref.1), custom_call_target="tpu_custom_call" | custom-call | tf_op jit(solution)/shard_map/pallas_call | solution.py:395
  64.6 0.0 copy-done
  64.7 0.0 copy-start.1
  64.7 1.8 %add.3 = f32[8,2,16,384]{3,2,1,0:T(8,128)} add(f32[8,2,16,384]{3,2,1,0:T(8,128)S(1)} %copy-done, f32[8,2,16,384]{3,2,1,0:T(8,128)} %bitcast.5) | non-fusion elementwise | flops 98304 | bytes 1179648 | tf_op jit(solution)/shard_map/add | solution.py:413
  66.5 0.0 copy-done.1
  66.5 0.6 copy.8
Async XLA Ops:
  0.6 64.0 %copy-start = (f32[8,2,16,384]{3,2,1,0:T(8,128)S(1)}, f32[8,2,16,384]{3,2,1,0:T(8,128)}, u32[]{:S(2)}) copy-start(f32[8,2,16,384]{3,2,1,0:T(8,128)} %param.5) | copy-start | bytes 1179652
  64.7 1.8 %copy-start.1 = (f32[8,1024]{1,0:T(8,128)S(1)}, f32[8,1024]{1,0:T(8,128)}, u32[]{:S(2)}) copy-start(f32[8,1024]{1,0:T(8,128)} %get-tuple-element.9) | copy-start | bytes 98308
